TPU v7x, 32 devices: a whole 2x2x4 slice. The times are simulated.
32 devices in a mesh: groups: 2 (over y), wide: 4 (over z), narrow: 4 (over x, core).
Axes of the slice: x: 2, y: 2, z: 4, core: 2. Of those that a mesh axis runs over, the one named last changes fastest.
Arguments:
- tokens: bfloat16 [128, 8192], P(('groups', 'wide'), 'narrow'), parts along dimension 0, may hold values from -60 to 60
- signs: int32 [128, 8192], P(('groups', 'wide'), 'narrow'), parts along dimension 0, may hold values 0 or 1
- magnitude: float32 [128, 8192], P(('groups', 'wide'), 'narrow'), parts along dimension 0, may hold values from 0.05 to 0.5
- target: bfloat16 [128, 8192], P(('groups', 'wide'), 'narrow'), parts along dimension 0, may hold values from -6 to 6
- norm_gain: float32 [8192], P('narrow'), may hold values from 0.1 to 1.9
- gate_weight: bfloat16 [8192, 20480], P('narrow', 'wide'), may hold values from -0.0625 to 0.0625
- up_weight: bfloat16 [8192, 20480], P('narrow', 'wide'), may hold values from -0.0625 to 0.0625
- down_weight: bfloat16 [20480, 8192], P('wide', 'narrow'), may hold values from -0.0390625 to 0.0390625
Outputs:
- new_delta: float32 [128, 8192], P(('groups', 'wide'), 'narrow'), parts along dimension 0
There are 2 independent parts, one for each index of `groups`. A program takes and returns all parts, laid end to end along the dimension named above; an argument that names none is the same for every part. Nothing has to cross between parts.
All inputs are finite; a program needn't handle non-finite values. No bound on the sum of `signs` on one device may be relied on, other than what follows from the above.
Results may differ from a plain program's by a relative error of at most 0.0034.
Values may be sent and summed in bfloat16 or wider, within the bound.
A program may use at most 192 MiB of HBM per device.

v0:
```python
import jax
import jax.numpy as jnp
from jax import lax
from jax.sharding import PartitionSpec as P

D = 8192


EPS = 1e-05
ASCENT = 0.5


def gate_terms(sums, hidden_width):
    gate = sums[:, :hidden_width]
    up = sums[:, hidden_width : 2 * hidden_width]
    back_hidden = sums[:, 2 * hidden_width :]
    sig = jax.nn.sigmoid(gate)
    back_gate = back_hidden * up * sig * (1.0 + gate * (1.0 - sig))
    back_up = back_hidden * gate * sig
    return jnp.concatenate([back_gate, back_up], axis=1).astype(jnp.bfloat16)


def on_device(tokens, signs, magnitude, target, norm_gain, gate_weight, up_weight, down_weight):
    hidden_width = gate_weight.shape[1]
    delta = (2 * signs - 1).astype(jnp.float32) * magnitude
    latent = tokens.astype(jnp.float32) + delta
    squares = lax.psum(jnp.sum(latent * latent, axis=1), "narrow")
    scale = lax.rsqrt(squares[:, None] / D + EPS)
    unit = latent * scale
    normed = (unit * norm_gain).astype(jnp.bfloat16)
    both_weights = jnp.concatenate([gate_weight, up_weight], axis=1)
    stacked = jnp.stack([normed, target], axis=0)
    piece = lax.all_gather(stacked, "wide", axis=1, tiled=True)
    forward = jnp.dot(piece[0], both_weights, preferred_element_type=jnp.float32)
    backward = lax.dot_general(
        piece[1], down_weight, (((1,), (1,)), ((), ())), preferred_element_type=jnp.float32
    )
    partial_value = jnp.concatenate([forward, backward], axis=1)
    shares = lax.psum_scatter(partial_value, "narrow", scatter_dimension=0, tiled=True)
    back_share = gate_terms(shares, hidden_width)
    back_both = lax.all_gather(back_share, "narrow", axis=0, tiled=True)
    piece = back_both
    back_normed = lax.psum_scatter(
        lax.dot_general(
            piece, both_weights, (((1,), (1,)), ((), ())), preferred_element_type=jnp.float32
        ),
        "wide",
        scatter_dimension=0,
        tiled=True,
    )
    scaled = back_normed * norm_gain
    inner = lax.psum(jnp.sum(scaled * unit, axis=1), "narrow")
    back_latent = scale * (scaled - unit * (inner[:, None] / D))
    return delta + ASCENT * (target.astype(jnp.float32) + back_latent)


def solution(mesh):
    in_specs = (
        P(("groups", "wide"), "narrow"),
        P(("groups", "wide"), "narrow"),
        P(("groups", "wide"), "narrow"),
        P(("groups", "wide"), "narrow"),
        P("narrow"),
        P("narrow", "wide"),
        P("narrow", "wide"),
        P("wide", "narrow"),
    )
    out_specs = P(("groups", "wide"), "narrow")
    return jax.shard_map(
        on_device, mesh=mesh, in_specs=in_specs, out_specs=out_specs, check_vma=False
    )
```

profile of v0, /device:TPU:0, one launch (start us, length us, event | category | flops | bytes accessed | tf_op | source)
XLA Modules:
  0.0 213.2 jit_solution(7017977959071597468)
XLA Ops:
  6.5 1.1 multiply_reduce_fusion.1
  7.7 8.4 %psum.14 = f32[16]{0:T(128)S(1)} all-reduce(f32[16]{0:T(128)S(1)} %get-tuple-element.5), channel_id=1, replica_groups=mesh['groups'=2,'wide'=4,'narrow'=4] {'narrow'}, use_global_device_ids=true, to_apply=%region_1.0 | all-reduce | flops 16 | bytes 128 | tf_op jit(solution)/shard_map/psum | solution.py:27
  16.1 0.9 fusion.5
  17.0 0.9 pad_maximum_fusion.2
  17.9 15.6 %all_gather.6 = bf16[2,64,2048]{2,1,0:T(8,128)(2,1)S(1)} all-gather(bf16[2,16,2048]{2,1,0:T(8,128)(2,1)S(1)} %pad_maximum_fusion.2), channel_id=1, replica_groups=mesh['groups'=2,'wide'=4,'narrow'=4] {'wide'}, dimensions={1}, use_global_device_ids=true | all-gather | bytes 655360 | tf_op jit(solution)/shard_map/all_gather | solution.py:33
  33.5 20.3 %constant_dynamic-update-slice_fusion.1 = bf16[2048,10240]{1,0:T(8,128)(2,1)} fusion(bf16[2048,5120]{1,0:T(8,128)(2,1)} %param.13), kind=kLoop, calls=%fused_computation.21 | loop fusion | bytes 41943040
  53.8 8.5 %constant_dynamic-update-slice_fusion = bf16[2048,10240]{1,0:T(8,128)(2,1)} fusion(bf16[2048,10240]{1,0:T(8,128)(2,1)} %constant_dynamic-update-slice_fusion.1, bf16[2048,5120]{1,0:T(8,128)(2,1)S(1)} %bitcast.14), kind=kLoop, calls=%fused_computation.20 | loop fusion | bytes 41943040 | tf_op jit(solution)/shard_map/concatenate | solution.py:31
  62.3 16.7 %fusion.4 = f32[64,10240]{1,0:T(8,128)S(1)} fusion(bf16[2048,10240]{1,0:T(8,128)(2,1)} %constant_dynamic-update-slice_fusion, bf16[2,64,2048]{2,1,0:T(8,128)(2,1)S(1)} %all_gather.6), kind=kOutput, calls=%fused_computation.11 | convolution fusion | flops 2684354560 | bytes 44826624 | tf_op jit(solution)/shard_map/dot_general | solution.py:34
  79.1 10.6 %fusion.3 = f32[64,5120]{1,0:T(8,128)S(1)} fusion(bf16[5120,2048]{1,0:T(8,128)(2,1)} %param.15, bf16[2,64,2048]{2,1,0:T(8,128)(2,1)S(1)} %all_gather.6), kind=kOutput, calls=%fused_computation.9 | convolution fusion | flops 1342177280 | bytes 22544384 | tf_op jit(solution)/shard_map/dot_general | solution.py:35
  89.7 2.1 %pad_maximum_fusion = f32[64,15360]{1,0:T(8,128)} fusion(f32[64,5120]{1,0:T(8,128)S(1)} %fusion.3, f32[64,10240]{1,0:T(8,128)S(1)} %fusion.4), kind=kLoop, calls=%fused_computation | loop fusion | flops 983040 | bytes 7864320 | tf_op jit(solution)/shard_map/concatenate | solution.py:38
  91.8 0.0 reduce-scatter.3.cloned.1.call-update
  91.8 0.0 all-gather.2.cloned.1.call-start
  91.9 44.1 %reduce-scatter.3.cloned.1.call-done = f32[16,15360]{1,0:T(8,128)} async-done(((f32[64,15360]{1,0:T(8,128)}), f32[16,15360]{1,0:T(8,128)}) %reduce-scatter.3.cloned.1.call-update) | async-done | bytes 983056 | tf_op jit(solution)/shard_map/reduce_scatter | solution.py:39
  136.0 1.3 fusion.2
  137.3 0.8 pad_maximum_fusion.1
  138.1 0.0 all-gather.2.cloned.1.call-update
  138.1 0.0 reduce-scatter.5.cloned.1.call-start
  138.2 18.2 %all-gather.2.cloned.1.call-done = bf16[64,10240]{1,0:T(8,128)(2,1)} async-done(((bf16[16,10240]{1,0:T(8,128)(2,1)}), bf16[64,10240]{1,0:T(8,128)(2,1)}) %all-gather.2.cloned.1.call-update) | async-done | bytes 1310736 | tf_op jit(solution)/shard_map/all_gather | solution.py:41
  156.4 19.8 %fusion.6 = f32[64,2048]{1,0:T(8,128)} fusion(bf16[64,10240]{1,0:T(8,128)(2,1)} %all-gather.2.cloned.1.call-done, bf16[2048,10240]{1,0:T(8,128)(2,1)} %constant_dynamic-update-slice_fusion), kind=kOutput, calls=%fused_computation.24 | convolution fusion | flops 2684354560 | bytes 43778048 | tf_op jit(solution)/shard_map/dot_general | solution.py:44
  176.2 0.0 reduce-scatter.5.cloned.1.call-update
  176.2 22.0 %reduce-scatter.5.cloned.1.call-done = f32[16,2048]{1,0:T(8,128)} async-done(((f32[64,2048]{1,0:T(8,128)}), f32[16,2048]{1,0:T(8,128)}) %reduce-scatter.5.cloned.1.call-update) | async-done | bytes 131088 | tf_op jit(solution)/shard_map/reduce_scatter | solution.py:43
  198.2 1.1 multiply_reduce_fusion
  199.3 5.7 %psum.15 = f32[16]{0:T(128)S(1)} all-reduce(f32[16]{0:T(128)S(1)} %multiply_reduce_fusion), channel_id=1, replica_groups=mesh['groups'=2,'wide'=4,'narrow'=4] {'narrow'}, use_global_device_ids=true, to_apply=%region_5.0 | all-reduce | flops 16 | bytes 128 | tf_op jit(solution)/shard_map/psum | solution.py:52
  205.0 1.7 multiply_add_fusion
  (20 shorter events, 0.1 us)
Async XLA Ops:
  6.5 129.5 %reduce-scatter.3.cloned.1.call-start = ((), (), s32[]{:S(2)}) async-start(), calls=%async_computation.2 | async-start | bytes 4915200 | tf_op jit(solution)/shard_map/reduce_scatter | solution.py:39
  17.8 35.9 %slice-start = ((s8[20971520]{0:T(1024)(128)(4,1)}), s8[4194304]{0:T(1024)(128)(4,1)S(1)}, s32[]{:S(2)}) async-start(s8[20971520]{0:T(1024)(128)(4,1)} %bitcast.13), calls=%async_computation.5 | async-start | bytes 8388608
  33.5 20.3 %slice-start.1 = ((s8[20971520]{0:T(1024)(128)(4,1)}), s8[4194304]{0:T(1024)(128)(4,1)S(1)}, s32[]{:S(2)}) async-start(s8[20971520]{0:T(1024)(128)(4,1)} %bitcast.13), calls=%async_computation.6 | async-start | bytes 8388608
  33.5 20.3 %slice-start.2 = ((s8[20971520]{0:T(1024)(128)(4,1)}), s8[4194304]{0:T(1024)(128)(4,1)S(1)}, s32[]{:S(2)}) async-start(s8[20971520]{0:T(1024)(128)(4,1)} %bitcast.13), calls=%async_computation.7 | async-start | bytes 8388608
  33.5 20.3 %slice-start.3 = ((s8[20971520]{0:T(1024)(128)(4,1)}), s8[4194304]{0:T(1024)(128)(4,1)S(1)}, s32[]{:S(2)}) async-start(s8[20971520]{0:T(1024)(128)(4,1)} %bitcast.13), calls=%async_computation.8 | async-start | bytes 8388608
  33.5 20.3 %slice-start.4 = ((s8[20971520]{0:T(1024)(128)(4,1)}), s8[4194304]{0:T(1024)(128)(4,1)S(1)}, s32[]{:S(2)}) async-start(s8[20971520]{0:T(1024)(128)(4,1)} %bitcast.13), calls=%async_computation.9 | async-start | bytes 8388608
  91.8 64.6 %all-gather.2.cloned.1.call-start = ((), (), s32[]{:S(2)}) async-start(), calls=%async_computation.3 | async-start | bytes 1638400 | tf_op jit(solution)/shard_map/all_gather | solution.py:41
  138.1 60.1 %copy-start = (bf16[16,2048]{1,0:T(8,128)(2,1)S(1)}, bf16[16,2048]{1,0:T(8,128)(2,1)}, u32[]{:S(2)}) copy-start(bf16[16,2048]{1,0:T(8,128)(2,1)} %param.8) | copy-start | bytes 196612
  138.1 60.1 %copy-start.2 = (f32[2048]{0:T(1024)S(1)}, f32[2048]{0:T(1024)}, u32[]{:S(2)}) copy-start(f32[2048]{0:T(1024)} %param.12) | copy-start | bytes 24580
  138.1 66.9 %copy-start.1 = (bf16[16,2048]{1,0:T(8,128)(2,1)S(1)}, bf16[16,2048]{1,0:T(8,128)(2,1)}, u32[]{:S(2)}) copy-start(bf16[16,2048]{1,0:T(8,128)(2,1)} %param.11) | copy-start | bytes 196612
  138.1 60.1 %reduce-scatter.5.cloned.1.call-start = ((), (), s32[]{:S(2)}) async-start(), calls=%async_computation.4 | async-start | bytes 655360 | tf_op jit(solution)/shard_map/reduce_scatter | solution.py:43
Sparse Core Ops, SparseCore 0:
  91.9 44.0 reduce-scatter.2
  138.2 18.1 all-gather.1
  176.4 21.8 reduce-scatter.4
where the time goes:
time: 214 us; the launch traced here: 213 us
  waiting for transfers between devices  84.4 us (39%)
  matrix products  47.1 us (22%)
  blocking collectives  29.6 us (14%)
  local copies, waits for them, and re-layouts  28.8 us (13%)
  between operations  13.2 us (6%)
  other arithmetic  9.93 us (5%)
    reduce_scatter x1, waiting for transfers between devices, on_device(): lax.psum_scatter(partial_value, 'narrow', scatter_dimension=0, tiled=True)  44.1 us
    reduce_scatter x1, waiting for transfers between devices, on_device(): lax.psum_scatter(lax.dot_general(piece, both_weights, (((1,), (1,)), ((),...  22 us
    unnamed x17, local copies, waits for them, and re-layouts  20.3 us
    dot_general x1, matrix products, on_device(): lax.dot_general(piece, both_weights, (((1,), (1,)), ((), ())), preferred_...  19.8 us
    all_gather x1, waiting for transfers between devices, on_device(): back_both = lax.all_gather(back_share, 'narrow', axis=0, tiled=True)  18.2 us
    dot_general x1, matrix products, on_device(): jnp.dot(piece[0], both_weights, preferred_element_type=jnp.float32)  16.7 us
    all_gather x1, blocking collectives, on_device(): piece = lax.all_gather(stacked, 'wide', axis=1, tiled=True)  15.6 us
    dot_general x1, matrix products, on_device(): lax.dot_general(piece[1], down_weight, (((1,), (1,)), ((), ())), preferre...  10.6 us
  transfers between devices with their start and end apart: 3, of which 3 were waited for; matrix products, arithmetic and copies ran while one was open for 0% of the time, Pallas kernels for 0%

commit v1 on v0

v1 whole, which is shorter than its diff:
```python
import functools
import jax
import jax.numpy as jnp
from jax import lax
from jax.experimental import pallas as pl
from jax.experimental.pallas import tpu as pltpu
from jax.sharding import PartitionSpec as P

EPS = 1e-05
ASCENT = 0.5
MESH = pl.DeviceIdType.MESH
BF = jnp.bfloat16
F32 = jnp.float32
NT = (((1,), (1,)), ((), ()))


def remote(src, dst, send_sem, recv_sem, axis, index):
    return pltpu.make_async_remote_copy(
        src_ref=src, dst_ref=dst, send_sem=send_sem, recv_sem=recv_sem,
        device_id={axis: index}, device_id_type=MESH,
    )


def plan(hidden):
    for chunks in (5, 4, 3, 2):
        if hidden % (chunks * 128) == 0:
            return chunks, hidden // chunks
    return 1, hidden


def kernel(
    dims, tok, sig, mag, tgt, gain, wg, wu, wd, out,
    wg_v, wu_v, wd_v, tg_all, xg_all, part, sq_s, sq_r, sc_own,
    a_cs, a_cr, a_own, a_xs, a_xr, b_cs, b_cr, b_own, b_xs, b_xr,
    bgu, in_all, in_r, acc, fs, fr,
    w_sem, d_sem, tg_ss, tg_rs, xg_ss, xg_rs, sq_ss, sq_rs,
    ac_ss, ac_rs, ax_ss, ax_rs, bc_ss, bc_rs, bx_ss, bx_rs,
    gx_ss, gx_rs, gc_ss, gc_rs, in_ss, in_rs, iw_ss, iw_rs, f_ss, f_rs,
):
    NW, X, C, chunks, hc, slots, pieces = dims
    nn = X * C
    Lt, Dl = tok.shape
    T = Lt * NW
    H = T // C
    R = T // nn
    D = Dl * nn
    w = lax.axis_index("wide")
    n = lax.axis_index("narrow")
    x, c = n // C, lax.rem(n, C)
    pc = lax.rem(c + 1, C)
    partner = x * C + pc
    block = c * X + x
    ctile = next(t for t in (512, 256, 128) if hc % t == 0)
    dtile = next(t for t in (512, 256, 128) if (Dl // pieces) % t == 0)
    sent = []

    def rows(i, size):
        return pl.ds(pl.multiple_of(i * size, size), size)

    def down_copy(k):
        return pltpu.make_async_copy(wd.at[pl.ds(k * hc, hc), :], wd_v.at[k % slots], d_sem.at[k % slots])

    def gu_copies(k):
        return (
            pltpu.make_async_copy(wg.at[:, pl.ds(k * hc, hc)], wg_v.at[k], w_sem.at[2 * k]),
            pltpu.make_async_copy(wu.at[:, pl.ds(k * hc, hc)], wu_v.at[k], w_sem.at[2 * k + 1]),
        )

    def go(cp):
        cp.start()
        sent.append(cp)

    for k in range(min(slots, chunks)):
        down_copy(k).start()
    for k in range(min(2, chunks)):
        for cp in gu_copies(k):
            cp.start()

    barrier = pltpu.get_barrier_semaphore()
    for k in range(1, NW):
        pl.semaphore_signal(barrier, inc=1, device_id={"wide": lax.rem(w + k, NW)}, device_id_type=MESH)
    for k in range(1, nn):
        pl.semaphore_signal(barrier, inc=1, device_id={"narrow": lax.rem(n + k, nn)}, device_id_type=MESH)
    pl.semaphore_wait(barrier, NW - 1 + nn - 1)

    mine = rows(w, Lt)
    for k in range(1, NW):
        go(remote(tgt, tg_all.at[mine], tg_ss.at[k - 1], tg_rs.at[k - 1], "wide", lax.rem(w + k, NW)))
    tg_all[mine, :] = tgt[...]
    latent = tok[...].astype(F32) + (2 * sig[...] - 1).astype(F32) * mag[...]
    sq_s[...] = jnp.broadcast_to(jnp.sum(latent * latent, axis=1, keepdims=True), (Lt, 128))
    for k in range(1, nn):
        go(remote(sq_s, sq_r.at[k - 1], sq_ss.at[k - 1], sq_rs.at[k - 1], "narrow", lax.rem(n + k, nn)))
    total = sq_s[...]
    for k in range(1, nn):
        remote(sq_s, sq_r.at[k - 1], sq_ss.at[k - 1], sq_rs.at[k - 1], "narrow", lax.rem(n + k, nn)).wait_recv()
        total = total + sq_r[k - 1]
    sc_own[...] = lax.rsqrt(total / D + EPS)
    latent = tok[...].astype(F32) + (2 * sig[...] - 1).astype(F32) * mag[...]
    xg_all[mine, :] = (latent * sc_own[...][:, :1] * gain[...]).astype(BF)
    for k in range(1, NW):
        go(remote(xg_all.at[mine], xg_all.at[mine], xg_ss.at[k - 1], xg_rs.at[k - 1], "wide", lax.rem(w + k, NW)))

    def wait_rows(dst, ss, rs, k):
        where = rows(lax.rem(w - k + NW, NW), Lt)
        remote(dst.at[where], dst.at[where], ss.at[k - 1], rs.at[k - 1], "wide", lax.rem(w + k, NW)).wait_recv()

    def stage1(k, width, cs, own, ss, rs, cr):
        own[k] = part[rows(c, H), pl.ds(0, width)]
        if C > 1:
            cs[k] = part[rows(pc, H), pl.ds(0, width)]
            go(remote(cs.at[k], cr.at[k], ss.at[k], rs.at[k], "narrow", partner))

    def stage2(k, cs, cr, own, css, crs, xs, xr, xss, xrs):
        if C > 1:
            remote(cs.at[k], cr.at[k], css.at[k], crs.at[k], "narrow", partner).wait_recv()
            own[k] = own[k] + cr[k]
        for j in range(1, X):
            to = lax.rem(x + j, X)
            xs[k, j - 1] = own[k, rows(to, R), :].astype(BF)
            s = k * (X - 1) + j - 1
            go(remote(xs.at[k, j - 1], xr.at[k, j - 1], xss.at[s], xrs.at[s], "narrow", to * C + c))

    def stage3(k, own, xs, xr, xss, xrs):
        for j in range(1, X):
            to = lax.rem(x + j, X)
            s = k * (X - 1) + j - 1
            remote(xs.at[k, j - 1], xr.at[k, j - 1], xss.at[s], xrs.at[s], "narrow", to * C + c).wait_recv()
        total = own[k, rows(x, R), :]
        for j in range(1, X):
            total = total + xr[k, j - 1].astype(F32)
        own[k, rows(x, R), :] = total

    brows = rows(block, R)

    def stage4(k):
        stage3(k, b_own, b_xs, b_xr, bx_ss, bx_rs)
        gate = b_own[k, rows(x, R), pl.ds(0, hc)]
        up = b_own[k, rows(x, R), pl.ds(hc, hc)]
        bh = a_own[k, rows(x, R), :]
        g = jax.nn.sigmoid(gate)
        bg = (bh * up * g * (1.0 + gate * (1.0 - g))).astype(BF)
        bu = (bh * gate * g).astype(BF)
        bgu[k, brows, pl.ds(0, hc)] = bg
        bgu[k, brows, pl.ds(hc, hc)] = bu
        got = jnp.broadcast_to(
            jnp.sum(bg.astype(F32) * gate + bu.astype(F32) * up, axis=1, keepdims=True), (R, 128)
        )
        in_all[brows, :] = got if k == 0 else in_all[brows, :] + got
        for j in range(1, X):
            q = k * (X - 1) + j - 1
            go(remote(bgu.at[k, brows], bgu.at[k, brows], gx_ss.at[q], gx_rs.at[q], "narrow", lax.rem(x + j, X) * C + c))
        if k == chunks - 1:
            for j in range(1, nn):
                go(remote(in_all.at[brows], in_all.at[brows], in_ss.at[j - 1], in_rs.at[j - 1], "narrow", lax.rem(n + j, nn)))

    def stage5(k):
        for j in range(1, X):
            q = k * (X - 1) + j - 1
            where = rows(c * X + lax.rem(x - j + X, X), R)
            remote(bgu.at[k, where], bgu.at[k, where], gx_ss.at[q], gx_rs.at[q], "narrow", lax.rem(x + j, X) * C + c).wait_recv()
        if C > 1:
            half = rows(c, H)
            go(remote(bgu.at[k, half], bgu.at[k, half], gc_ss.at[k], gc_rs.at[k], "narrow", partner))

    def stage6(k):
        if C > 1:
            half = rows(pc, H)
            remote(bgu.at[k, half], bgu.at[k, half], gc_ss.at[k], gc_rs.at[k], "narrow", partner).wait_recv()

    def inner_stage():
        for j in range(1, nn):
            other = lax.rem(n - j + nn, nn)
            where = rows(lax.rem(other, C) * X + other // C, R)
            remote(in_all.at[where], in_all.at[where], in_ss.at[j - 1], in_rs.at[j - 1], "narrow", lax.rem(n + j, nn)).wait_recv()
        for k in range(1, NW):
            to = lax.rem(w + k, NW)
            go(remote(in_all.at[rows(to, Lt)], in_r.at[k - 1], iw_ss.at[k - 1], iw_rs.at[k - 1], "wide", to))

    tasks = [("A", k) for k in range(chunks)] + [("B", k) for k in range(chunks)] + [("C", k) for k in range(chunks)]
    order = {t: i for i, t in enumerate(tasks)}
    after = {i: [] for i in range(len(tasks) + 4)}
    for k in range(chunks):
        i = order[("A", k)]
        after[i].append(lambda k=k: stage1(k, hc, a_cs, a_own, ac_ss, ac_rs, a_cr))
        after[i + 1].append(lambda k=k: stage2(k, a_cs, a_cr, a_own, ac_ss, ac_rs, a_xs, a_xr, ax_ss, ax_rs))
        after[i + 2].append(lambda k=k: stage3(k, a_own, a_xs, a_xr, ax_ss, ax_rs))
    for k in range(chunks):
        i = order[("B", k)]
        after[i].append(lambda k=k: stage1(k, 2 * hc, b_cs, b_own, bc_ss, bc_rs, b_cr))
        after[i + 1].append(lambda k=k: stage2(k, b_cs, b_cr, b_own, bc_ss, bc_rs, b_xs, b_xr, bx_ss, bx_rs))
        after[i + 2].append(lambda k=k: stage4(k))
        after[i + 3].append(lambda k=k: stage5(k))

    def final_send(p):
        width = Dl // pieces
        cols = pl.ds(p * width, width)
        for k in range(1, NW):
            to = lax.rem(w + k, NW)
            q = (k - 1) * pieces + p
            fs[k - 1, :, cols] = acc[rows(to, Lt), cols].astype(BF)
            go(remote(fs.at[k - 1, :, cols], fr.at[k - 1, :, cols], f_ss.at[q], f_rs.at[q], "wide", to))

    done = set()

    def run_after(i):
        if i in done:
            return
        done.add(i)
        for f in reversed(after[i]):
            f()

    for i, (kind, k) in enumerate(tasks):
        if kind == "A":
            if k == 0:
                for j in range(1, NW):
                    wait_rows(tg_all, tg_ss, tg_rs, j)
            down_copy(k).wait()
            if k + 2 < chunks:
                for cp in gu_copies(k + 2):
                    cp.start()

            @pl.loop(0, hc // ctile)
            def _(t):
                cols = rows(t, ctile)
                part[:, cols] = lax.dot_general(
                    tg_all[...], wd_v[k % slots, cols, :], NT, preferred_element_type=F32
                )

            if k + slots < chunks:
                down_copy(k + slots).start()
        elif kind == "B":
            if k == 0:
                for j in range(1, NW):
                    wait_rows(xg_all, xg_ss, xg_rs, j)
            for cp in gu_copies(k):
                cp.wait()

            @pl.loop(0, hc // ctile)
            def _(t):
                part[:, rows(t, ctile)] = jnp.dot(
                    xg_all[...], wg_v[k, :, rows(t, ctile)], preferred_element_type=F32
                )
                part[:, pl.ds(pl.multiple_of(hc + t * ctile, ctile), ctile)] = jnp.dot(
                    xg_all[...], wu_v[k, :, rows(t, ctile)], preferred_element_type=F32
                )
        else:
            for q in range(i):
                run_after(q)
            if order[("B", k)] + 3 >= i:
                for q in range(i, order[("B", k)] + 4):
                    run_after(q)
            stage6(k)
            last = k == chunks - 1
            if last:
                for q in sorted(after):
                    run_after(q)
                inner_stage()
            per = (Dl // dtile) // pieces
            for p in range(pieces if last else 1):
                lo, hi = (p * per, (p + 1) * per) if last else (0, Dl // dtile)

                @pl.loop(lo, hi)
                def _(t):
                    cols = rows(t, dtile)
                    got = lax.dot_general(
                        bgu[k, :, pl.ds(0, hc)], wg_v[k, cols, :], NT, preferred_element_type=F32
                    ) + lax.dot_general(
                        bgu[k, :, pl.ds(hc, hc)], wu_v[k, cols, :], NT, preferred_element_type=F32
                    )
                    if k == 0:
                        acc[:, cols] = got
                    else:
                        acc[:, cols] = acc[:, cols] + got

                if last:
                    final_send(p)
        run_after(i)

    inner = in_all[mine, :]
    for k in range(1, NW):
        to = lax.rem(w + k, NW)
        remote(in_all.at[rows(to, Lt)], in_r.at[k - 1], iw_ss.at[k - 1], iw_rs.at[k - 1], "wide", to).wait_recv()
        inner = inner + in_r[k - 1]
    scale = sc_own[...][:, :1]
    mean = inner[:, :1] / D
    width = Dl // pieces
    for p in range(pieces):
        cols = pl.ds(p * width, width)
        total = acc[mine, cols]
        for k in range(1, NW):
            to = lax.rem(w + k, NW)
            q = (k - 1) * pieces + p
            remote(fs.at[k - 1, :, cols], fr.at[k - 1, :, cols], f_ss.at[q], f_rs.at[q], "wide", to).wait_recv()
            total = total + fr[k - 1, :, cols].astype(F32)
        delta = (2 * sig[:, cols] - 1).astype(F32) * mag[:, cols]
        unit = (tok[:, cols].astype(F32) + delta) * scale
        back = scale * (total * gain[:, cols] - unit * mean)
        out[:, cols] = delta + ASCENT * (tgt[:, cols].astype(F32) + back)
    for cp in sent:
        cp.wait_send()


def on_device(NW, nn, tokens, signs, magnitude, target, norm_gain, gate_weight, up_weight, down_weight):
    Lt, Dl = tokens.shape
    hidden = gate_weight.shape[1]
    T = Lt * NW
    C = 2 if nn % 2 == 0 else 1
    X = nn // C
    chunks, hc = plan(hidden)
    slots = min(3, chunks)
    pieces = 4 if Dl % 512 == 0 else 1
    H, R = T // C, T // nn
    dims = (NW, X, C, chunks, hc, slots, pieces)
    V = pltpu.VMEM
    S = lambda k: pltpu.SemaphoreType.DMA((max(k, 1),))
    mw, mn, mx = NW - 1, nn - 1, X - 1
    scratch = [
        V((chunks, Dl, hc), BF), V((chunks, Dl, hc), BF), V((slots, hc, Dl), BF),
        V((T, Dl), BF), V((T, Dl), BF), V((T, 2 * hc), F32),
        V((Lt, 128), F32), V((max(mn, 1), Lt, 128), F32), V((Lt, 128), F32),
        V((chunks, H, hc), F32), V((chunks, H, hc), F32), V((chunks, H, hc), F32),
        V((chunks, max(mx, 1), R, hc), BF), V((chunks, max(mx, 1), R, hc), BF),
        V((chunks, H, 2 * hc), F32), V((chunks, H, 2 * hc), F32), V((chunks, H, 2 * hc), F32),
        V((chunks, max(mx, 1), R, 2 * hc), BF), V((chunks, max(mx, 1), R, 2 * hc), BF),
        V((chunks, T, 2 * hc), BF), V((T, 128), F32), V((max(mw, 1), Lt, 128), F32),
        V((T, Dl), F32), V((max(mw, 1), Lt, Dl), BF), V((max(mw, 1), Lt, Dl), BF),
        S(2 * chunks), S(slots),
        S(mw), S(mw), S(mw), S(mw), S(mn), S(mn),
        S(chunks), S(chunks), S(chunks * mx), S(chunks * mx),
        S(chunks), S(chunks), S(chunks * mx), S(chunks * mx),
        S(chunks * mx), S(chunks * mx), S(chunks), S(chunks),
        S(mn), S(mn), S(mw), S(mw), S(mw * pieces), S(mw * pieces),
    ]
    vm = pl.BlockSpec(memory_space=pltpu.VMEM)
    hbm = pl.BlockSpec(memory_space=pl.ANY)
    return pl.pallas_call(
        functools.partial(kernel, dims),
        out_shape=jax.ShapeDtypeStruct((Lt, Dl), F32),
        in_specs=[vm] * 5 + [hbm] * 3,
        out_specs=vm,
        scratch_shapes=scratch,
        compiler_params=pltpu.CompilerParams(
            collective_id=0, has_side_effects=True, vmem_limit_bytes=67043328
        ),
    )(tokens, signs, magnitude, target, norm_gain.reshape(1, Dl), gate_weight, up_weight, down_weight)


def solution(mesh):
    in_specs = (
        P(("groups", "wide"), "narrow"),
        P(("groups", "wide"), "narrow"),
        P(("groups", "wide"), "narrow"),
        P(("groups", "wide"), "narrow"),
        P("narrow"),
        P("narrow", "wide"),
        P("narrow", "wide"),
        P("wide", "narrow"),
    )
    return jax.shard_map(
        functools.partial(on_device, mesh.shape["wide"], mesh.shape["narrow"]),
        mesh=mesh, in_specs=in_specs, out_specs=P(("groups", "wide"), "narrow"), check_vma=False,
    )
```

time: 214 us -> 63.4 us (0.30)
  waiting for transfers between devices: 84.4 us -> 0 us
  Pallas kernels: 0 us -> 61.6 us
  matrix products: 47.1 us -> 0 us
  blocking collectives: 29.6 us -> 0 us
  local copies, waits for them, and re-layouts: 28.8 us -> 1.57 us
  between operations: 13.2 us -> 0.01 us
  other arithmetic: 9.93 us -> 0 us
    reduce_scatter x2 -> x0, waiting for transfers between devices: 66.1 us -> none  [the longest x1 44.1 us: on_device(): lax.psum_scatter(partial_value, 'narrow', scatter_dimension=0, tiled=True)]
    pallas_call x0 -> x1, Pallas kernels: none -> 61.6 us  [on_device(): pl.pallas_call(functools.partial(kernel, dims), out_shape=jax.ShapeDtypeS...]
    dot_general x3 -> x0, matrix products: 47.1 us -> none  [the longest x1 19.8 us: on_device(): lax.dot_general(piece, both_weights, (((1,), (1,)), ((), ())), preferred_...]
    unnamed x17 -> x1, local copies, waits for them, and re-layouts: 20.3 us -> 1.57 us
    all_gather x1 -> x0, waiting for transfers between devices: 18.2 us -> none  [on_device(): back_both = lax.all_gather(back_share, 'narrow', axis=0, tiled=True)]
    all_gather x1 -> x0, blocking collectives: 15.6 us -> none  [on_device(): piece = lax.all_gather(stacked, 'wide', axis=1, tiled=True)]
    psum x2 -> x0, blocking collectives: 14 us -> none  [the longest x1 8.37 us: on_device(): squares = lax.psum(jnp.sum(latent * latent, axis=1), 'narrow')]
    concatenate x1 -> x0, local copies, waits for them, and re-layouts: 8.54 us -> none  [on_device(): both_weights = jnp.concatenate([gate_weight, up_weight], axis=1)]
  transfers between devices with their start and end apart: 3 -> 0, of which waited for: 3 -> 0; matrix products, arithmetic and copies ran while one was open for 0% -> 0% of each run, Pallas kernels for 0% -> 0%
where the time goes in v1:
time: 63.4 us; the launch traced here: 63.2 us
  Pallas kernels  61.6 us (97%)
  local copies, waits for them, and re-layouts  1.57 us (2%)
    pallas_call x1, Pallas kernels, on_device(): pl.pallas_call(functools.partial(kernel, dims), out_shape=jax.ShapeDtypeS...  61.6 us
    unnamed x1, local copies, waits for them, and re-layouts  1.57 us

profile of v1, /device:TPU:0, one launch (start us, length us, event | category | flops | bytes accessed | tf_op | source)
XLA Modules:
  0.0 63.2 jit_solution(18078865925288890327)
XLA Ops:
  0.0 61.6 %shard_map.82 = f32[16,2048]{1,0:T(8,128)} custom-call(bf16[16,2048]{1,0:T(8,128)(2,1)} %tok.1, s32[16,2048]{1,0:T(8,128)} %sig.1, f32[16,2048]{1,0:T(8,128)} %mag.1, bf16[16,2048]{1,0:T(8,128)(2,1)} %tgt.1, f32[1,2048]{1,0:T(1,128)} %bitcast.1, bf16[2048,5120]{1,0:T(8,128)(2,1)} %wg.1, bf16[2048,5120]{1,0:T(8,128)(2,1)} %wu.1, bf16[5120,2048]{1,0:T(8,128)(2,1)} %wd.1), custom_call_target="tpu_custom_call" | custom-call | tf_op jit(solution)/shard_map/pallas_call | solution.py:337
  61.7 1.6 %copy.10 = f32[16,2048]{1,0:T(8,128)} copy(f32[16,2048]{1,0:T(8,128)} %shard_map.82) | data formatting | bytes 262144

commit v2 on v1

--- a/solution.py
+++ b/solution.py
@@ -32,19 +32,23 @@
     dims, tok, sig, mag, tgt, gain, wg, wu, wd, out,
     wg_v, wu_v, wd_v, tg_all, xg_all, part, sq_s, sq_r, sc_own,
     a_cs, a_cr, a_own, a_xs, a_xr, b_cs, b_cr, b_own, b_xs, b_xr,
-    bgu, in_all, in_r, acc, fs, fr,
+    bgu, in_all, in_r, acc, fs, fr, in_s, iy_r, ys, yr,
     w_sem, d_sem, tg_ss, tg_rs, xg_ss, xg_rs, sq_ss, sq_rs,
     ac_ss, ac_rs, ax_ss, ax_rs, bc_ss, bc_rs, bx_ss, bx_rs,
     gx_ss, gx_rs, gc_ss, gc_rs, in_ss, in_rs, iw_ss, iw_rs, f_ss, f_rs,
+    ty_ss, ty_rs, xy_ss, xy_rs, iy_ss, iy_rs, y_ss, y_rs,
 ):
-    NW, X, C, chunks, hc, slots, pieces = dims
+    G, NW, X, C, chunks, hc, slots, ahead, pieces = dims
     nn = X * C
     Lt, Dl = tok.shape
-    T = Lt * NW
+    T = Lt * NW * G
     H = T // C
     R = T // nn
     D = Dl * nn
     w = lax.axis_index("wide")
+    g = lax.axis_index("groups") if G > 1 else 0
+    own_w = g * NW + w
+    base = g * (chunks * hc)
     n = lax.axis_index("narrow")
     x, c = n // C, lax.rem(n, C)
     pc = lax.rem(c + 1, C)
@@ -57,13 +61,16 @@
     def rows(i, size):
         return pl.ds(pl.multiple_of(i * size, size), size)
 
+    def hidden_cols(k):
+        return pl.ds(pl.multiple_of(base + k * hc, 128), hc)
+
     def down_copy(k):
-        return pltpu.make_async_copy(wd.at[pl.ds(k * hc, hc), :], wd_v.at[k % slots], d_sem.at[k % slots])
+        return pltpu.make_async_copy(wd.at[hidden_cols(k), :], wd_v.at[k % slots], d_sem.at[k % slots])
 
     def gu_copies(k):
         return (
-            pltpu.make_async_copy(wg.at[:, pl.ds(k * hc, hc)], wg_v.at[k], w_sem.at[2 * k]),
-            pltpu.make_async_copy(wu.at[:, pl.ds(k * hc, hc)], wu_v.at[k], w_sem.at[2 * k + 1]),
+            pltpu.make_async_copy(wg.at[:, hidden_cols(k)], wg_v.at[k], w_sem.at[2 * k]),
+            pltpu.make_async_copy(wu.at[:, hidden_cols(k)], wu_v.at[k], w_sem.at[2 * k + 1]),
         )
 
     def go(cp):
@@ -72,7 +79,7 @@
 
     for k in range(min(slots, chunks)):
         down_copy(k).start()
-    for k in range(min(2, chunks)):
+    for k in range(min(ahead, chunks)):
         for cp in gu_copies(k):
             cp.start()
 
@@ -81,11 +88,28 @@
         pl.semaphore_signal(barrier, inc=1, device_id={"wide": lax.rem(w + k, NW)}, device_id_type=MESH)
     for k in range(1, nn):
         pl.semaphore_signal(barrier, inc=1, device_id={"narrow": lax.rem(n + k, nn)}, device_id_type=MESH)
-    pl.semaphore_wait(barrier, NW - 1 + nn - 1)
-
-    mine = rows(w, Lt)
+    for k in range(1, G):
+        pl.semaphore_signal(barrier, inc=1, device_id={"groups": lax.rem(g + k, G)}, device_id_type=MESH)
+    pl.semaphore_wait(barrier, NW - 1 + nn - 1 + G - 1)
+
+    mine = rows(own_w, Lt)
+
+    def share(src, dst, k, ss, rs):
+        where = rows(g * NW + lax.rem(w - k + NW, NW), Lt)
+        for j in range(1, G):
+            q = (j - 1) * NW + k
+            go(remote(src if k == 0 else dst.at[where], dst.at[where], ss.at[q], rs.at[q], "groups", lax.rem(g + j, G)))
+
+    def wait_shared(dst, ss, rs):
+        for k in range(NW):
+            for j in range(1, G):
+                q = (j - 1) * NW + k
+                where = rows(lax.rem(g - j + G, G) * NW + lax.rem(w - k + NW, NW), Lt)
+                remote(dst.at[where], dst.at[where], ss.at[q], rs.at[q], "groups", lax.rem(g + j, G)).wait_recv()
+
     for k in range(1, NW):
         go(remote(tgt, tg_all.at[mine], tg_ss.at[k - 1], tg_rs.at[k - 1], "wide", lax.rem(w + k, NW)))
+    share(tgt, tg_all, 0, ty_ss, ty_rs)
     tg_all[mine, :] = tgt[...]
     latent = tok[...].astype(F32) + (2 * sig[...] - 1).astype(F32) * mag[...]
     sq_s[...] = jnp.broadcast_to(jnp.sum(latent * latent, axis=1, keepdims=True), (Lt, 128))
@@ -100,9 +124,10 @@
     xg_all[mine, :] = (latent * sc_own[...][:, :1] * gain[...]).astype(BF)
     for k in range(1, NW):
         go(remote(xg_all.at[mine], xg_all.at[mine], xg_ss.at[k - 1], xg_rs.at[k - 1], "wide", lax.rem(w + k, NW)))
+    share(xg_all.at[mine], xg_all, 0, xy_ss, xy_rs)
 
     def wait_rows(dst, ss, rs, k):
-        where = rows(lax.rem(w - k + NW, NW), Lt)
+        where = rows(g * NW + lax.rem(w - k + NW, NW), Lt)
         remote(dst.at[where], dst.at[where], ss.at[k - 1], rs.at[k - 1], "wide", lax.rem(w + k, NW)).wait_recv()
 
     def stage1(k, width, cs, own, ss, rs, cr):
@@ -173,9 +198,21 @@
             other = lax.rem(n - j + nn, nn)
             where = rows(lax.rem(other, C) * X + other // C, R)
             remote(in_all.at[where], in_all.at[where], in_ss.at[j - 1], in_rs.at[j - 1], "narrow", lax.rem(n + j, nn)).wait_recv()
+        for j in range(1, G):
+            to = lax.rem(g + j, G)
+            go(remote(in_all.at[rows(to, Lt * NW)], iy_r.at[j - 1], iy_ss.at[j - 1], iy_rs.at[j - 1], "groups", to))
+
+    def inner_wide():
+        ours = rows(g, Lt * NW)
+        total = in_all[ours, :]
+        for j in range(1, G):
+            to = lax.rem(g + j, G)
+            remote(in_all.at[rows(to, Lt * NW)], iy_r.at[j - 1], iy_ss.at[j - 1], iy_rs.at[j - 1], "groups", to).wait_recv()
+            total = total + iy_r[j - 1]
+        in_s[...] = total
         for k in range(1, NW):
             to = lax.rem(w + k, NW)
-            go(remote(in_all.at[rows(to, Lt)], in_r.at[k - 1], iw_ss.at[k - 1], iw_rs.at[k - 1], "wide", to))
+            go(remote(in_s.at[rows(to, Lt)], in_r.at[k - 1], iw_ss.at[k - 1], iw_rs.at[k - 1], "wide", to))
 
     tasks = [("A", k) for k in range(chunks)] + [("B", k) for k in range(chunks)] + [("C", k) for k in range(chunks)]
     order = {t: i for i, t in enumerate(tasks)}
@@ -192,13 +229,28 @@
         after[i + 2].append(lambda k=k: stage4(k))
         after[i + 3].append(lambda k=k: stage5(k))
 
+    def final_groups(p):
+        width = Dl // pieces
+        cols = pl.ds(p * width, width)
+        for j in range(1, G):
+            to = lax.rem(g + j, G)
+            q = (j - 1) * pieces + p
+            ys[j - 1, :, cols] = acc[rows(to, Lt * NW), cols].astype(BF)
+            go(remote(ys.at[j - 1, :, cols], yr.at[j - 1, :, cols], y_ss.at[q], y_rs.at[q], "groups", to))
+
     def final_send(p):
         width = Dl // pieces
         cols = pl.ds(p * width, width)
+        ours = rows(g, Lt * NW)
+        for j in range(1, G):
+            to = lax.rem(g + j, G)
+            q = (j - 1) * pieces + p
+            remote(ys.at[j - 1, :, cols], yr.at[j - 1, :, cols], y_ss.at[q], y_rs.at[q], "groups", to).wait_recv()
+            acc[ours, cols] = acc[ours, cols] + yr[j - 1, :, cols].astype(F32)
         for k in range(1, NW):
             to = lax.rem(w + k, NW)
             q = (k - 1) * pieces + p
-            fs[k - 1, :, cols] = acc[rows(to, Lt), cols].astype(BF)
+            fs[k - 1, :, cols] = acc[rows(g * NW + to, Lt), cols].astype(BF)
             go(remote(fs.at[k - 1, :, cols], fr.at[k - 1, :, cols], f_ss.at[q], f_rs.at[q], "wide", to))
 
     done = set()
@@ -215,9 +267,11 @@
             if k == 0:
                 for j in range(1, NW):
                     wait_rows(tg_all, tg_ss, tg_rs, j)
+                    share(None, tg_all, j, ty_ss, ty_rs)
+                wait_shared(tg_all, ty_ss, ty_rs)
             down_copy(k).wait()
-            if k + 2 < chunks:
-                for cp in gu_copies(k + 2):
+            if k + ahead < chunks:
+                for cp in gu_copies(k + ahead):
                     cp.start()
 
             @pl.loop(0, hc // ctile)
@@ -229,10 +283,13 @@
 
             if k + slots < chunks:
                 down_copy(k + slots).start()
-        elif kind == "B":
             if k == 0:
                 for j in range(1, NW):
                     wait_rows(xg_all, xg_ss, xg_rs, j)
+                    share(None, xg_all, j, xy_ss, xy_rs)
+        elif kind == "B":
+            if k == 0:
+                wait_shared(xg_all, xy_ss, xy_rs)
             for cp in gu_copies(k):
                 cp.wait()
 
@@ -274,13 +331,18 @@
                         acc[:, cols] = acc[:, cols] + got
 
                 if last:
-                    final_send(p)
+                    final_groups(p)
+                    if p > 0:
+                        final_send(p - 1)
+            if last:
+                final_send(pieces - 1)
+                inner_wide()
         run_after(i)
 
-    inner = in_all[mine, :]
+    inner = in_s[rows(w, Lt), :]
     for k in range(1, NW):
         to = lax.rem(w + k, NW)
-        remote(in_all.at[rows(to, Lt)], in_r.at[k - 1], iw_ss.at[k - 1], iw_rs.at[k - 1], "wide", to).wait_recv()
+        remote(in_s.at[rows(to, Lt)], in_r.at[k - 1], iw_ss.at[k - 1], iw_rs.at[k - 1], "wide", to).wait_recv()
         inner = inner + in_r[k - 1]
     scale = sc_own[...][:, :1]
     mean = inner[:, :1] / D
@@ -301,17 +363,19 @@
         cp.wait_send()
 
 
-def on_device(NW, nn, tokens, signs, magnitude, target, norm_gain, gate_weight, up_weight, down_weight):
+def on_device(groups, NW, nn, tokens, signs, magnitude, target, norm_gain, gate_weight, up_weight, down_weight):
     Lt, Dl = tokens.shape
     hidden = gate_weight.shape[1]
-    T = Lt * NW
+    G = groups if hidden % (groups * 128) == 0 else 1
+    T = Lt * NW * G
     C = 2 if nn % 2 == 0 else 1
     X = nn // C
-    chunks, hc = plan(hidden)
-    slots = min(3, chunks)
+    chunks, hc = plan(hidden // G)
+    slots = chunks if G > 1 else min(3, chunks)
+    ahead = chunks if G > 1 else 2
     pieces = 4 if Dl % 512 == 0 else 1
     H, R = T // C, T // nn
-    dims = (NW, X, C, chunks, hc, slots, pieces)
+    dims = (G, NW, X, C, chunks, hc, slots, ahead, pieces)
     V = pltpu.VMEM
     S = lambda k: pltpu.SemaphoreType.DMA((max(k, 1),))
     mw, mn, mx = NW - 1, nn - 1, X - 1
@@ -325,12 +389,16 @@
         V((chunks, max(mx, 1), R, 2 * hc), BF), V((chunks, max(mx, 1), R, 2 * hc), BF),
         V((chunks, T, 2 * hc), BF), V((T, 128), F32), V((max(mw, 1), Lt, 128), F32),
         V((T, Dl), F32), V((max(mw, 1), Lt, Dl), BF), V((max(mw, 1), Lt, Dl), BF),
+        V((Lt * NW, 128), F32), V((max(G - 1, 1), Lt * NW, 128), F32),
+        V((max(G - 1, 1), Lt * NW, Dl), BF), V((max(G - 1, 1), Lt * NW, Dl), BF),
         S(2 * chunks), S(slots),
         S(mw), S(mw), S(mw), S(mw), S(mn), S(mn),
         S(chunks), S(chunks), S(chunks * mx), S(chunks * mx),
         S(chunks), S(chunks), S(chunks * mx), S(chunks * mx),
         S(chunks * mx), S(chunks * mx), S(chunks), S(chunks),
         S(mn), S(mn), S(mw), S(mw), S(mw * pieces), S(mw * pieces),
+        S((G - 1) * NW), S((G - 1) * NW), S((G - 1) * NW), S((G - 1) * NW),
+        S(G - 1), S(G - 1), S((G - 1) * pieces), S((G - 1) * pieces),
     ]
     vm = pl.BlockSpec(memory_space=pltpu.VMEM)
     hbm = pl.BlockSpec(memory_space=pl.ANY)
@@ -358,6 +426,6 @@
         P("wide", "narrow"),
     )
     return jax.shard_map(
-        functools.partial(on_device, mesh.shape["wide"], mesh.shape["narrow"]),
+        functools.partial(on_device, mesh.shape["groups"], mesh.shape["wide"], mesh.shape["narrow"]),
         mesh=mesh, in_specs=in_specs, out_specs=P(("groups", "wide"), "narrow"), check_vma=False,
     )

time: 63.4 us -> 69 us (1.088)
  Pallas kernels: 61.6 us -> 67.3 us
    pallas_call x1, Pallas kernels: 61.6 us -> 67.3 us  [on_device(): pl.pallas_call(functools.partial(kernel, dims), out_shape=jax.ShapeDtypeS...]
where the time goes in v2:
time: 69 us; the launch traced here: 68.9 us
  Pallas kernels  67.3 us (98%)
  local copies, waits for them, and re-layouts  1.57 us (2%)
    pallas_call x1, Pallas kernels, on_device(): pl.pallas_call(functools.partial(kernel, dims), out_shape=jax.ShapeDtypeS...  67.3 us
    unnamed x1, local copies, waits for them, and re-layouts  1.57 us

profile of v2, /device:TPU:0, one launch (start us, length us, event | category | flops | bytes accessed | tf_op | source)
XLA Modules:
  0.0 68.9 jit_solution(13995341435374392789)
XLA Ops:
  0.0 67.3 %shard_map.82 = f32[16,2048]{1,0:T(8,128)} custom-call(bf16[16,2048]{1,0:T(8,128)(2,1)} %tok.1, s32[16,2048]{1,0:T(8,128)} %sig.1, f32[16,2048]{1,0:T(8,128)} %mag.1, bf16[16,2048]{1,0:T(8,128)(2,1)} %tgt.1, f32[1,2048]{1,0:T(1,128)} %bitcast.1, bf16[2048,5120]{1,0:T(8,128)(2,1)} %wg.1, bf16[2048,5120]{1,0:T(8,128)(2,1)} %wu.1, bf16[5120,2048]{1,0:T(8,128)(2,1)} %wd.1), custom_call_target="tpu_custom_call" | custom-call | tf_op jit(solution)/shard_map/pallas_call | solution.py:405
  67.3 1.6 %copy.10 = f32[16,2048]{1,0:T(8,128)} copy(f32[16,2048]{1,0:T(8,128)} %shard_map.82) | data formatting | bytes 262144
